TPU v7x, 256 devices: a whole 4x4x8 slice. The times are simulated.
256 devices in a mesh: layer: 8 (over z_lo, core), feat: 32 (over x, y, z_hi).
Axes of the slice: x: 4, y: 4, z: 8 (z_hi: 2, z_lo: 4; z = z_hi * 4 + z_lo), core: 2. Of those that a mesh axis runs over, the one named last changes fastest.
Arguments:
- source: bfloat16 [512, 2304], P('feat', 'layer'), may hold values from -6 to 6
- enc_weight: bfloat16 [2304, 32768], P('layer', 'feat'), may hold values from -0.125 to 0.125
- enc_bias: float32 [32768], P('feat'), may hold values from -3 to 3
- dec_weight: bfloat16 [8, 32768, 2304], P('layer', 'feat'), may hold values from -0.03125 to 0.03125
- dec_bias: float32 [8, 2304], P('layer'), may hold values from -3 to 3
- targets: bfloat16 [8, 512, 2304], P('layer', 'feat'), may hold values from -6 to 6
Outputs:
- enc_grad: bfloat16 [2304, 32768], P('layer', 'feat')
- dec_grad: bfloat16 [8, 32768, 2304], P('layer', 'feat')
All inputs are finite; a program needn't handle non-finite values.
Results may differ from a plain program's by a relative error of at most 0.014.
Values may be sent and summed in bfloat16 or wider, within the bound.
A program may use at most 64 MiB of HBM per device.

v0:
```python
import jax
import jax.numpy as jnp
from jax import lax
from jax.sharding import PartitionSpec as P


def body(source, enc_weight, enc_bias, dec_weight, dec_bias, targets):
    source_rows = lax.all_gather(source, "feat", axis=0, tiled=True)
    partial_input = jnp.dot(source_rows, enc_weight, preferred_element_type=jnp.float32)
    preact = lax.psum(partial_input, "layer")
    preact = preact + enc_bias[None, :]
    active = jnp.maximum(preact, 0.0)
    features = (active * active).astype(jnp.bfloat16)
    decoder = dec_weight[0]
    picked = features
    rebuilt = lax.psum_scatter(
        jnp.dot(picked, decoder, preferred_element_type=jnp.float32).astype(jnp.bfloat16),
        "feat",
        scatter_dimension=0,
        tiled=True,
    ).astype(jnp.float32)
    rebuilt = rebuilt + dec_bias[0][None, :]
    residual = (rebuilt - targets[0].astype(jnp.float32)).astype(jnp.bfloat16)
    piece = lax.all_gather(residual, "feat", axis=0, tiled=True)
    picked = features
    weight_total = lax.dot_general(
        picked, piece, (((0,), (0,)), ((), ())), preferred_element_type=jnp.float32
    )
    grad_block = lax.dot_general(
        piece, decoder, (((1,), (1,)), ((), ())), preferred_element_type=jnp.float32
    )
    grad_total = grad_block
    weight_total, grad_total = (weight_total, grad_total)
    summed = lax.psum(grad_total, "layer")
    feat_grad = (2.0 * active * summed).astype(jnp.bfloat16)
    enc_grad = lax.dot_general(
        source_rows, feat_grad, (((0,), (0,)), ((), ())), preferred_element_type=jnp.float32
    ).astype(jnp.bfloat16)
    return (enc_grad, weight_total.astype(jnp.bfloat16)[None])


def solution(mesh):
    placed = (
        P("feat", "layer"),
        P("layer", "feat"),
        P("feat"),
        P("layer", "feat", None),
        P("layer", None),
        P("layer", "feat", None),
    )
    return jax.shard_map(
        body,
        mesh=mesh,
        in_specs=placed,
        out_specs=(P("layer", "feat"), P("layer", "feat", None)),
        check_vma=False,
    )
```

profile of v0, /device:TPU:2, one launch (start us, length us, event | category | flops | bytes accessed | tf_op | source)
XLA Modules:
  0.0 654.4 jit_solution(1544659206685551485)
XLA Ops:
  7.2 0.0 copy-start
  7.2 0.0 all-reduce.3.cloned.1.call-start
  7.2 110.1 %all_gather.6 = bf16[512,288]{1,0:T(8,128)(2,1)S(1)} all-gather(bf16[16,288]{1,0:T(8,128)(2,1)} %param.6), channel_id=1, replica_groups=mesh['layer'=8,'feat'=32] {'feat'}, dimensions={0}, use_global_device_ids=true | all-gather | bytes 304128 | tf_op jit(solution)/shard_map/all_gather | solution.py:8
  117.4 0.0 copy-done
  117.4 2.0 fusion.17
  119.4 0.0 all-reduce.3.cloned.1.call-update
  119.4 0.0 reduce-scatter.2.cloned.1.call-start
  119.5 84.3 %all-reduce.3.cloned.1.call-done = f32[512,1024]{1,0:T(8,128)} async-done(((f32[512,1024]{1,0:T(8,128)}), f32[512,1024]{1,0:T(8,128)}) %all-reduce.3.cloned.1.call-update) | async-done | bytes 2097168 | tf_op jit(solution)/shard_map/psum | solution.py:10
  203.8 0.0 copy-done.4
  203.8 7.0 %fusion.5 = bf16[512,2304]{1,0:T(8,128)(2,1)} fusion(bf16[1,1024,2304]{2,1,0:T(8,128)(2,1)} %param.9, f32[512,1024]{1,0:T(8,128)} %all-reduce.3.cloned.1.call-done, f32[1024]{0:T(1024)S(1)} %copy-done.4), kind=kOutput, calls=%fused_computation.6 | convolution fusion | flops 2419195904 | bytes 9179136 | tf_op jit(solution)/shard_map/dot_general | solution.py:17
  210.8 0.0 reduce-scatter.2.cloned.1.call-update
  210.8 0.0 all-gather.2.cloned.1.call-start
  210.9 0.6 copy-done.3
  211.5 259.3 %reduce-scatter.2.cloned.1.call-done = bf16[16,2304]{1,0:T(8,128)(2,1)} async-done(((bf16[512,2304]{1,0:T(8,128)(2,1)}), bf16[16,2304]{1,0:T(8,128)(2,1)}) %reduce-scatter.2.cloned.1.call-update) | async-done | bytes 73744 | tf_op jit(solution)/shard_map/reduce_scatter | solution.py:16
  470.9 1.5 fusion.12
  472.4 0.0 all-gather.2.cloned.1.call-update
  472.5 0.0 all-reduce.5.cloned.1.call-start
  472.5 90.1 %all-gather.2.cloned.1.call-done = bf16[512,2304]{1,0:T(8,128)(2,1)} async-done(((bf16[16,2304]{1,0:T(8,128)(2,1)}), bf16[512,2304]{1,0:T(8,128)(2,1)}) %all-gather.2.cloned.1.call-update) | async-done | bytes 2359312 | tf_op jit(solution)/shard_map/all_gather | solution.py:24
  562.6 7.1 %fusion.1 = f32[512,1024]{1,0:T(8,128)} fusion(bf16[512,2304]{1,0:T(8,128)(2,1)} %all-gather.2.cloned.1.call-done, bf16[1,1024,2304]{2,1,0:T(8,128)(2,1)} %param.9), kind=kOutput, calls=%fused_computation.2 | convolution fusion | flops 2415919104 | bytes 9175040 | tf_op jit(solution)/shard_map/dot_general | solution.py:29
  569.7 0.0 all-reduce.5.cloned.1.call-update
  569.7 1.6 copy-done.1
  571.3 6.0 fusion
  577.2 67.6 %all-reduce.5.cloned.1.call-done = f32[512,1024]{1,0:T(8,128)} async-done(((f32[512,1024]{1,0:T(8,128)}), f32[512,1024]{1,0:T(8,128)}) %all-reduce.5.cloned.1.call-update) | async-done | bytes 2097168 | tf_op jit(solution)/shard_map/psum | solution.py:34
  644.9 3.0 fusion.8
  (6 shorter events, 0.0 us)
Async XLA Ops:
  7.2 110.2 %copy-start = (bf16[288,1024]{1,0:T(8,128)(2,1)S(1)}, bf16[288,1024]{1,0:T(8,128)(2,1)}, u32[]{:S(2)}) copy-start(bf16[288,1024]{1,0:T(8,128)(2,1)} %param.7) | copy-start | bytes 1769476
  7.2 196.6 %all-reduce.3.cloned.1.call-start = ((), (), s32[]{:S(2)}) async-start(), calls=%async_computation.1 | async-start | bytes 4194304 | tf_op jit(solution)/shard_map/psum | solution.py:10
  117.4 86.4 %copy-start.4 = (f32[1024]{0:T(1024)S(1)}, f32[1024]{0:T(1024)}, u32[]{:S(2)}) copy-start(f32[1024]{0:T(1024)} %param.8) | copy-start | bytes 12292
  119.4 351.5 %reduce-scatter.2.cloned.1.call-start = ((), (), s32[]{:S(2)}) async-start(), calls=%async_computation.2 | async-start | bytes 2433024 | tf_op jit(solution)/shard_map/reduce_scatter | solution.py:16
  210.8 0.7 copy-start.3
  210.8 260.1 %copy-start.2 = (bf16[1,16,2304]{2,1,0:T(8,128)(2,1)S(1)}, bf16[1,16,2304]{2,1,0:T(8,128)(2,1)}, u32[]{:S(2)}) copy-start(bf16[1,16,2304]{2,1,0:T(8,128)(2,1)} %param.11) | copy-start | bytes 221188
  210.8 351.8 %all-gather.2.cloned.1.call-start = ((), (), s32[]{:S(2)}) async-start(), calls=%async_computation.3 | async-start | bytes 2433024 | tf_op jit(solution)/shard_map/all_gather | solution.py:24
  472.5 172.4 %all-reduce.5.cloned.1.call-start = ((), (), s32[]{:S(2)}) async-start(), calls=%async_computation.4 | async-start | bytes 4194304 | tf_op jit(solution)/shard_map/psum | solution.py:34
  569.7 1.6 copy-start.1
Sparse Core Ops, SparseCore 0:
  119.5 84.2 all-reduce.2
  211.0 259.8 reduce-scatter.1
  474.9 87.7 all-gather.1
  569.8 75.0 all-reduce.4
where the time goes:
time: 655 us; the launch traced here: 654 us
  waiting for transfers between devices  501 us (76%)
  blocking collectives  110 us (17%)
  matrix products  25.1 us (4%)
  between operations  13.8 us (2%)
    reduce_scatter x1, waiting for transfers between devices, body(): lax.psum_scatter(jnp.dot(picked, decoder, preferred_element_type=jnp.floa...  259 us
    all_gather x1, blocking collectives, body(): source_rows = lax.all_gather(source, 'feat', axis=0, tiled=True)  110 us
    all_gather x1, waiting for transfers between devices, body(): piece = lax.all_gather(residual, 'feat', axis=0, tiled=True)  90.1 us
    psum x1, waiting for transfers between devices, body(): preact = lax.psum(partial_input, 'layer')  84.3 us
    psum x1, waiting for transfers between devices, body(): summed = lax.psum(grad_total, 'layer')  67.6 us
  transfers between devices with their start and end apart: 4, of which 4 were waited for; matrix products, arithmetic and copies ran while one was open for 1% of the time, Pallas kernels for 0%

commit v1 on v0

--- a/solution.py
+++ b/solution.py
@@ -4,8 +4,16 @@
 from jax.sharding import PartitionSpec as P
 
 
+def replace_the_trees(a0, k_dim):
+    g_now = lax.all_to_all(
+        jnp.stack([a0 for _ in range(lax.axis_size("feat"))], axis=0), "feat", 0, 0
+    )
+    u_next = jnp.concatenate(g_now, axis=k_dim)
+    return u_next
+
+
 def body(source, enc_weight, enc_bias, dec_weight, dec_bias, targets):
-    source_rows = lax.all_gather(source, "feat", axis=0, tiled=True)
+    source_rows = replace_the_trees(source, 0)
     partial_input = jnp.dot(source_rows, enc_weight, preferred_element_type=jnp.float32)
     preact = lax.psum(partial_input, "layer")
     preact = preact + enc_bias[None, :]

time: 655 us -> 567 us (0.87)
  blocking collectives: 110 us -> 27.5 us
    all_gather x1 -> x0, blocking collectives: 110 us -> none  [body(): source_rows = lax.all_gather(source, 'feat', axis=0, tiled=True)]
    all_to_all x0 -> x1, blocking collectives: none -> 27.5 us  [replace_the_trees(): lax.all_to_all(jnp.stack([a0 for _ in range(lax.axis_size('feat'))], axis...]
where the time goes in v1:
time: 567 us
  waiting for transfers between devices  496 us (87%)
  blocking collectives  27.5 us (5%)
  matrix products  25.1 us (4%)
  between operations  13.8 us (2%)
    reduce_scatter x1, waiting for transfers between devices, body(): lax.psum_scatter(jnp.dot(picked, decoder, preferred_element_type=jnp.floa...  259 us
    all_gather x1, waiting for transfers between devices, body(): piece = lax.all_gather(residual, 'feat', axis=0, tiled=True)  90.2 us
    psum x1, waiting for transfers between devices, body(): preact = lax.psum(partial_input, 'layer')  78.9 us
    psum x1, waiting for transfers between devices, body(): summed = lax.psum(grad_total, 'layer')  67.6 us
    all_to_all x1, blocking collectives, replace_the_trees(): lax.all_to_all(jnp.stack([a0 for _ in range(lax.axis_size('feat'))], axis...  27.5 us
  transfers between devices with their start and end apart: 4, of which 4 were waited for; matrix products, arithmetic and copies ran while one was open for 1% of the time, Pallas kernels for 0%

profile of v1, /device:TPU:2, one launch (start us, length us, event | category | flops | bytes accessed | tf_op | source)
XLA Modules:
  0.0 567.1 jit_solution(16231936883823019276)
XLA Ops:
  7.2 0.0 copy-start
  7.2 0.0 all-reduce.3.cloned.1.call-start
  7.2 0.8 stack.2
  8.0 27.5 %all_to_all.5 = bf16[32,16,288]{2,1,0:T(8,128)(2,1)S(1)} all-to-all(bf16[32,16,288]{2,1,0:T(8,128)(2,1)S(1)} %stack.2), channel_id=1, replica_groups=mesh['layer'=8,'feat'=32] {'feat'}, dimensions={0} | all-to-all | bytes 589824 | tf_op jit(solution)/shard_map/all_to_all | solution.py:8
  35.5 0.0 copy-done
  35.5 2.0 fusion.17
  37.5 0.0 all-reduce.3.cloned.1.call-update
  37.6 0.0 reduce-scatter.2.cloned.1.call-start
  37.6 78.9 %all-reduce.3.cloned.1.call-done = f32[512,1024]{1,0:T(8,128)} async-done(((f32[512,1024]{1,0:T(8,128)}), f32[512,1024]{1,0:T(8,128)}) %all-reduce.3.cloned.1.call-update) | async-done | bytes 2097168 | tf_op jit(solution)/shard_map/psum | solution.py:18
  116.5 7.0 %fusion.5 = bf16[512,2304]{1,0:T(8,128)(2,1)} fusion(bf16[1,1024,2304]{2,1,0:T(8,128)(2,1)} %param.9, f32[512,1024]{1,0:T(8,128)} %all-reduce.3.cloned.1.call-done, f32[1024]{0:T(1024)S(1)} %copy-done.4), kind=kOutput, calls=%fused_computation.6 | convolution fusion | flops 2419195904 | bytes 9179136 | tf_op jit(solution)/shard_map/dot_general | solution.py:25
  123.5 0.0 reduce-scatter.2.cloned.1.call-update
  123.5 0.0 all-gather.2.cloned.1.call-start
  123.6 0.6 copy-done.3
  124.2 259.3 %reduce-scatter.2.cloned.1.call-done = bf16[16,2304]{1,0:T(8,128)(2,1)} async-done(((bf16[512,2304]{1,0:T(8,128)(2,1)}), bf16[16,2304]{1,0:T(8,128)(2,1)}) %reduce-scatter.2.cloned.1.call-update) | async-done | bytes 73744 | tf_op jit(solution)/shard_map/reduce_scatter | solution.py:24
  383.5 1.5 fusion.12
  385.1 0.0 all-gather.2.cloned.1.call-update
  385.1 0.0 all-reduce.5.cloned.1.call-start
  385.1 90.2 %all-gather.2.cloned.1.call-done = bf16[512,2304]{1,0:T(8,128)(2,1)} async-done(((bf16[16,2304]{1,0:T(8,128)(2,1)}), bf16[512,2304]{1,0:T(8,128)(2,1)}) %all-gather.2.cloned.1.call-update) | async-done | bytes 2359312 | tf_op jit(solution)/shard_map/all_gather | solution.py:32
  475.3 7.1 %fusion.1 = f32[512,1024]{1,0:T(8,128)} fusion(bf16[512,2304]{1,0:T(8,128)(2,1)} %all-gather.2.cloned.1.call-done, bf16[1,1024,2304]{2,1,0:T(8,128)(2,1)} %param.9), kind=kOutput, calls=%fused_computation.2 | convolution fusion | flops 2415919104 | bytes 9175040 | tf_op jit(solution)/shard_map/dot_general | solution.py:37
  482.4 0.0 all-reduce.5.cloned.1.call-update
  482.4 1.6 copy-done.1
  484.0 6.0 %fusion = bf16[1,1024,2304]{2,1,0:T(8,128)(2,1)} fusion(bf16[512,2304]{1,0:T(8,128)(2,1)} %all-gather.2.cloned.1.call-done, f32[512,1024]{1,0:T(8,128)S(1)} %copy-done.1, f32[1024]{0:T(1024)S(1)} %copy-done.4), kind=kOutput, calls=%fused_computation.1 | convolution fusion | flops 2420375552 | bytes 9179136 | tf_op jit(solution)/shard_map/dot_general | solution.py:34
  489.9 67.6 %all-reduce.5.cloned.1.call-done = f32[512,1024]{1,0:T(8,128)} async-done(((f32[512,1024]{1,0:T(8,128)}), f32[512,1024]{1,0:T(8,128)}) %all-reduce.5.cloned.1.call-update) | async-done | bytes 2097168 | tf_op jit(solution)/shard_map/psum | solution.py:42
  557.5 3.0 fusion.8
  (7 shorter events, 0.0 us)
Async XLA Ops:
  7.2 28.3 %copy-start = (bf16[288,1024]{1,0:T(8,128)(2,1)S(1)}, bf16[288,1024]{1,0:T(8,128)(2,1)}, u32[]{:S(2)}) copy-start(bf16[288,1024]{1,0:T(8,128)(2,1)} %param.7) | copy-start | bytes 1769476
  7.2 109.3 %all-reduce.3.cloned.1.call-start = ((), (), s32[]{:S(2)}) async-start(), calls=%async_computation.2 | async-start | bytes 4194304 | tf_op jit(solution)/shard_map/psum | solution.py:18
  35.5 81.0 %copy-start.4 = (f32[1024]{0:T(1024)S(1)}, f32[1024]{0:T(1024)}, u32[]{:S(2)}) copy-start(f32[1024]{0:T(1024)} %param.8) | copy-start | bytes 12292
  37.6 345.9 %reduce-scatter.2.cloned.1.call-start = ((), (), s32[]{:S(2)}) async-start(), calls=%async_computation.3 | async-start | bytes 2433024 | tf_op jit(solution)/shard_map/reduce_scatter | solution.py:24
  123.5 0.7 copy-start.3
  123.5 260.0 %copy-start.2 = (bf16[1,16,2304]{2,1,0:T(8,128)(2,1)S(1)}, bf16[1,16,2304]{2,1,0:T(8,128)(2,1)}, u32[]{:S(2)}) copy-start(bf16[1,16,2304]{2,1,0:T(8,128)(2,1)} %param.11) | copy-start | bytes 221188
  123.5 351.8 %all-gather.2.cloned.1.call-start = ((), (), s32[]{:S(2)}) async-start(), calls=%async_computation.4 | async-start | bytes 2433024 | tf_op jit(solution)/shard_map/all_gather | solution.py:32
  385.1 172.5 %all-reduce.5.cloned.1.call-start = ((), (), s32[]{:S(2)}) async-start(), calls=%async_computation.5 | async-start | bytes 4194304 | tf_op jit(solution)/shard_map/psum | solution.py:42
  482.4 1.6 copy-start.1
Sparse Core Ops, SparseCore 0:
  37.7 78.7 all-reduce.2
  123.6 259.8 reduce-scatter.1
  387.5 87.7 all-gather.1
  482.5 74.9 all-reduce.4
